TPU v7x, 256 devices: a whole 4x4x8 slice. The times are simulated.
256 devices in a mesh: inb: 16 (over x, y), outb: 16 (over z, core).
Axes of the slice: x: 4, y: 4, z: 8, core: 2. Of those that a mesh axis runs over, the one named last changes fastest.
Arguments:
- tokens: bfloat16 [512, 8192], P('outb', 'inb'), may hold values from -6 to 6
- grad_out: bfloat16 [512, 8192], P('outb', 'inb'), may hold values from -6 to 6
- gate_weight: bfloat16 [8192, 28672], P('inb', 'outb'), may hold values from -0.09375 to 0.09375
- up_weight: bfloat16 [8192, 28672], P('inb', 'outb'), may hold values from -0.09375 to 0.09375
- down_weight: bfloat16 [28672, 8192], P('outb', 'inb'), may hold values from -0.046875 to 0.046875
- gate_mask: int32 [64, 224], P('inb', 'outb'), may hold values 0 or 1
- up_mask: int32 [64, 224], P('inb', 'outb'), may hold values 0 or 1
- down_mask: int32 [224, 64], P('outb', 'inb'), may hold values 0 or 1
Outputs:
- layer_out: bfloat16 [512, 8192], P('outb', 'inb')
- grad_tokens: bfloat16 [512, 8192], P('outb', 'inb')
- grad_gate: bfloat16 [8192, 28672], P('inb', 'outb')
- grad_up: bfloat16 [8192, 28672], P('inb', 'outb')
- grad_down: bfloat16 [28672, 8192], P('outb', 'inb')
All inputs are finite; a program needn't handle non-finite values. No bound on the sum of `gate_mask` or of `up_mask` or of `down_mask` on one device may be relied on, other than what follows from the above.
Results may differ from a plain program's by a relative error of at most 0.0049.
Values may be sent and summed in bfloat16 or wider, within the bound.
A program may use at most 128 MiB of HBM per device.

v0:
```python
import jax
import jax.numpy as jnp
from jax import lax
from jax.sharding import PartitionSpec as P


def expand(weight, mask):
    rows, cols = mask.shape
    side_rows = weight.shape[0] // rows
    side_cols = weight.shape[1] // cols
    blocks = weight.reshape(rows, side_rows, cols, side_cols)
    return (blocks * mask.astype(weight.dtype)[:, None, :, None]).reshape(weight.shape)


def times_transpose(left, right):
    return lax.dot_general(
        left, right, (((1,), (1,)), ((), ())), preferred_element_type=jnp.float32
    )


def transpose_times(left, right):
    return lax.dot_general(
        left, right, (((0,), (0,)), ((), ())), preferred_element_type=jnp.float32
    )


def swiglu_grad(hidden_grad, gate, up):
    sigmoid_gate = jax.nn.sigmoid(gate)
    gate_grad = (hidden_grad * up * sigmoid_gate * (1.0 + gate * (1.0 - sigmoid_gate))).astype(
        jnp.bfloat16
    )
    up_grad = (hidden_grad * gate * sigmoid_gate).astype(jnp.bfloat16)
    return (gate_grad, up_grad)


def swiglu(gate, up):
    return (gate * jax.nn.sigmoid(gate) * up).astype(jnp.bfloat16)


def local(tokens, grad_out, gate_weight, up_weight, down_weight, gate_mask, up_mask, down_mask):
    gate_sparse = expand(gate_weight, gate_mask)
    up_sparse = expand(up_weight, up_mask)
    down_sparse = expand(down_weight, down_mask)
    tokens_all = lax.all_gather(tokens, "outb", axis=0, tiled=True)
    cotangent_all = lax.all_gather(grad_out, "outb", axis=0, tiled=True)
    gate_part = jnp.dot(tokens_all, gate_sparse, preferred_element_type=jnp.float32)
    up_part = jnp.dot(tokens_all, up_sparse, preferred_element_type=jnp.float32)
    gate, up = (
        lax.psum_scatter(gate_part, "inb", scatter_dimension=1, tiled=True),
        lax.psum_scatter(up_part, "inb", scatter_dimension=1, tiled=True),
    )
    hidden = swiglu(gate, up)
    hidden_all = lax.all_gather(hidden, "inb", axis=1, tiled=True)
    hidden_part = times_transpose(cotangent_all, down_sparse)
    hidden_grad = lax.psum_scatter(hidden_part, "inb", scatter_dimension=1, tiled=True)
    gate_grad, up_grad = swiglu_grad(hidden_grad, gate, up)
    gate_grad_all, up_grad_all = (
        lax.all_gather(gate_grad, "inb", axis=1, tiled=True),
        lax.all_gather(up_grad, "inb", axis=1, tiled=True),
    )
    layer_out = lax.psum_scatter(
        jnp.dot(hidden_all, down_sparse, preferred_element_type=jnp.float32),
        "outb",
        scatter_dimension=0,
        tiled=True,
    ).astype(jnp.bfloat16)
    grad_tokens = lax.psum_scatter(
        times_transpose(gate_grad_all, gate_sparse) + times_transpose(up_grad_all, up_sparse),
        "outb",
        scatter_dimension=0,
        tiled=True,
    ).astype(jnp.bfloat16)
    grad_gate = expand(transpose_times(tokens_all, gate_grad_all), gate_mask).astype(jnp.bfloat16)
    grad_up = expand(transpose_times(tokens_all, up_grad_all), up_mask).astype(jnp.bfloat16)
    grad_down = expand(transpose_times(hidden_all, cotangent_all), down_mask).astype(jnp.bfloat16)
    return (layer_out, grad_tokens, grad_gate, grad_up, grad_down)


def solution(mesh):
    return jax.shard_map(
        local,
        mesh=mesh,
        in_specs=(
            P("outb", "inb"),
            P("outb", "inb"),
            P("inb", "outb"),
            P("inb", "outb"),
            P("outb", "inb"),
            P("inb", "outb"),
            P("inb", "outb"),
            P("outb", "inb"),
        ),
        out_specs=(
            P("outb", "inb"),
            P("outb", "inb"),
            P("inb", "outb"),
            P("inb", "outb"),
            P("outb", "inb"),
        ),
        check_vma=False,
    )
```

profile of v0, /device:TPU:1, one launch (start us, length us, event | category | flops | bytes accessed | tf_op | source)
XLA Modules:
  0.0 563.5 jit_solution(647137082323829711)
XLA Ops:
  7.2 23.0 %all_gather.15 = bf16[512,512]{1,0:T(8,128)(2,1)S(1)} all-gather(bf16[32,512]{1,0:T(8,128)(2,1)} %param.8), channel_id=1, replica_groups=mesh['inb'=16,'outb'=16] {'outb'}, dimensions={0}, use_global_device_ids=true | all-gather | bytes 557056 | tf_op jit(solution)/shard_map/all_gather | solution.py:44
  31.1 2.8 copy.20
  35.7 3.0 convolution_bitcast_fusion.2
  39.4 3.8 copy.22
  45.1 3.0 convolution_bitcast_fusion.1
  48.9 16.0 %all_gather.17 = bf16[512,512]{1,0:T(8,128)(2,1)S(1)} all-gather(bf16[32,512]{1,0:T(8,128)(2,1)S(1)} %copy-done.9), channel_id=1, replica_groups=mesh['inb'=16,'outb'=16] {'outb'}, dimensions={0}, use_global_device_ids=true | all-gather | bytes 557056 | tf_op jit(solution)/shard_map/all_gather | solution.py:45
  66.7 3.1 convolution_bitcast_fusion
  69.9 46.5 %reduce-scatter.6.cloned.1.call-done = f32[512,112]{0,1:T(8,128)} async-done(((f32[512,1792]{0,1:T(8,128)}), f32[512,112]{0,1:T(8,128)}) %reduce-scatter.6.cloned.1.call-update) | async-done | bytes 229392 | tf_op jit(solution)/shard_map/reduce_scatter | solution.py:49
  116.3 84.4 %reduce-scatter.8.cloned.1.call-done = f32[512,112]{0,1:T(8,128)} async-done(((f32[512,1792]{0,1:T(8,128)}), f32[512,112]{0,1:T(8,128)}) %reduce-scatter.8.cloned.1.call-update) | async-done | bytes 229392 | tf_op jit(solution)/shard_map/reduce_scatter | solution.py:50
  200.7 84.5 %reduce-scatter.12.cloned.1.call-done = f32[512,112]{0,1:T(8,128)} async-done(((f32[512,1792]{0,1:T(8,128)}), f32[512,112]{0,1:T(8,128)}) %reduce-scatter.12.cloned.1.call-update) | async-done | bytes 229392 | tf_op jit(solution)/shard_map/reduce_scatter | solution.py:55
  285.2 2.0 multiply_convert_fusion
  288.5 48.3 %all-gather.6.cloned.1.call-done = bf16[512,1792]{0,1:T(8,128)(2,1)} async-done(((bf16[512,112]{0,1:T(8,128)(2,1)}), bf16[512,1792]{0,1:T(8,128)(2,1)}) %all-gather.6.cloned.1.call-update) | async-done | bytes 1835024 | tf_op jit(solution)/shard_map/all_gather | solution.py:58
  336.8 4.2 fusion.3
  341.0 47.0 %all-gather.8.cloned.1.call-done = bf16[512,1792]{0,1:T(8,128)(2,1)} async-done(((bf16[512,112]{0,1:T(8,128)(2,1)}), bf16[512,1792]{0,1:T(8,128)(2,1)}) %all-gather.8.cloned.1.call-update) | async-done | bytes 1835024 | tf_op jit(solution)/shard_map/all_gather | solution.py:59
  388.0 5.0 convolution_add_fusion
  393.2 45.9 %all-gather.4.cloned.1.call-done = bf16[512,1792]{0,1:T(8,128)(2,1)} async-done(((bf16[512,112]{0,1:T(8,128)(2,1)}), bf16[512,1792]{0,1:T(8,128)(2,1)}) %all-gather.4.cloned.1.call-update) | async-done | bytes 1835024 | tf_op jit(solution)/shard_map/all_gather | solution.py:53
  439.1 4.2 fusion.4
  446.3 2.4 copy.27
  451.3 2.4 copy.28
  455.2 2.3 fusion
  457.6 39.2 %reduce-scatter.14.cloned.1.call-done = f32[32,512]{1,0:T(8,128)} async-done(((f32[512,512]{1,0:T(8,128)}), f32[32,512]{1,0:T(8,128)}) %reduce-scatter.14.cloned.1.call-update) | async-done | bytes 65552 | tf_op jit(solution)/shard_map/reduce_scatter | solution.py:67
  496.7 1.5 convert_element_type.49
  498.2 57.0 %reduce-scatter.10.cloned.1.call-done = f32[32,512]{1,0:T(8,128)} async-done(((f32[512,512]{1,0:T(8,128)}), f32[32,512]{1,0:T(8,128)}) %reduce-scatter.10.cloned.1.call-update) | async-done | bytes 65552 | tf_op jit(solution)/shard_map/reduce_scatter | solution.py:61
  555.2 1.5 convert_element_type.46
  (57 shorter events, 16.3 us)
Async XLA Ops:
  7.2 109.2 %reduce-scatter.6.cloned.1.call-start = ((), (), s32[]{:S(2)}) async-start(), calls=%async_computation.5 | async-start | bytes 3899392 | tf_op jit(solution)/shard_map/reduce_scatter | solution.py:49
  34.4 1.2 copy-start
  38.6 0.7 copy-start.10
  38.7 162.1 %reduce-scatter.8.cloned.1.call-start = ((), (), s32[]{:S(2)}) async-start(), calls=%async_computation.6 | async-start | bytes 3899392 | tf_op jit(solution)/shard_map/reduce_scatter | solution.py:50
  43.3 1.8 copy-start.1
  43.8 1.3 copy-start.2
  48.1 0.7 copy-start.11
  48.1 0.8 copy-start.9
  48.1 237.1 %reduce-scatter.12.cloned.1.call-start = ((), (), s32[]{:S(2)}) async-start(), calls=%async_computation.9 | async-start | bytes 3899392 | tf_op jit(solution)/shard_map/reduce_scatter | solution.py:55
  48.9 17.8 %copy-start.5 = (bf16[1792,512]{1,0:T(8,128)(2,1)S(1)}, bf16[1792,512]{1,0:T(8,128)(2,1)}, u32[]{:S(2)}) copy-start(bf16[1792,512]{1,0:T(8,128)(2,1)} %param.12) | copy-start | bytes 5505028
  65.5 1.2 copy-start.3
  69.8 267.0 %all-gather.6.cloned.1.call-start = ((), (), s32[]{:S(2)}) async-start(), calls=%async_computation.10 | async-start | bytes 1949696 | tf_op jit(solution)/shard_map/all_gather | solution.py:58
  287.3 100.7 %all-gather.8.cloned.1.call-start = ((), (), s32[]{:S(2)}) async-start(), calls=%async_computation.11 | async-start | bytes 1949696 | tf_op jit(solution)/shard_map/all_gather | solution.py:59
  287.9 151.3 %all-gather.4.cloned.1.call-start = ((), (), s32[]{:S(2)}) async-start(), calls=%async_computation.7 | async-start | bytes 1949696 | tf_op jit(solution)/shard_map/all_gather | solution.py:53
  288.4 208.3 %reduce-scatter.14.cloned.1.call-start = ((), (), s32[]{:S(2)}) async-start(), calls=%async_computation.12 | async-start | bytes 1114112 | tf_op jit(solution)/shard_map/reduce_scatter | solution.py:67
  341.0 98.1 %copy-start.4 = (bf16[14,128,4,128]{3,2,1,0:T(4,128)(2,1)S(1)}, bf16[14,128,4,128]{3,2,1,0:T(4,128)(2,1)}, u32[]{:S(2)}) copy-start(bf16[14,128,4,128]{3,2,1,0:T(4,128)(2,1)} %copy-done.3) | copy-start | bytes 5505028
  393.0 162.2 %reduce-scatter.10.cloned.1.call-start = ((), (), s32[]{:S(2)}) async-start(), calls=%async_computation.8 | async-start | bytes 1114112 | tf_op jit(solution)/shard_map/reduce_scatter | solution.py:61
  443.6 1.5 copy-start.6
  448.7 1.5 copy-start.8
  453.7 1.5 copy-start.7
Sparse Core Ops, SparseCore 0:
  38.8 77.4 reduce-scatter.5
  120.0 80.7 reduce-scatter.7
  204.4 80.7 reduce-scatter.11
  287.5 49.2 all-gather.5
  339.1 48.7 all-gather.7
  390.3 48.7 all-gather.3
  441.6 55.0 reduce-scatter.13
  499.4 55.7 reduce-scatter.9
where the time goes:
time: 566 us; the launch traced here: 563 us
  waiting for transfers between devices  454 us (80%)
  blocking collectives  39 us (7%)
  matrix products  27 us (5%)
  local copies, waits for them, and re-layouts  23.1 us (4%)
  between operations  14.2 us (3%)
  other arithmetic  5.73 us (1%)
    reduce_scatter x1, waiting for transfers between devices, local(): lax.psum_scatter(hidden_part, 'inb', scatter_dimension=1, tiled=True)  84.5 us
    reduce_scatter x1, waiting for transfers between devices, local(): lax.psum_scatter(up_part, 'inb', scatter_dimension=1, tiled=True)  84.4 us
    reduce_scatter x1, waiting for transfers between devices, local(): lax.psum_scatter(jnp.dot(hidden_all, down_sparse, preferred_element_type=...  57 us
    all_gather x1, waiting for transfers between devices, local(): lax.all_gather(gate_grad, 'inb', axis=1, tiled=True)  48.3 us
    all_gather x1, waiting for transfers between devices, local(): lax.all_gather(up_grad, 'inb', axis=1, tiled=True)  47 us
    reduce_scatter x1, waiting for transfers between devices, local(): lax.psum_scatter(gate_part, 'inb', scatter_dimension=1, tiled=True)  46.5 us
    all_gather x1, waiting for transfers between devices, local(): hidden_all = lax.all_gather(hidden, 'inb', axis=1, tiled=True)  45.9 us
    reduce_scatter x1, waiting for transfers between devices, local(): lax.psum_scatter(times_transpose(gate_grad_all, gate_sparse) + times_tran...  39.2 us
  transfers between devices with their start and end apart: 8, of which 8 were waited for; matrix products, arithmetic and copies ran while one was open for 7% of the time, Pallas kernels for 0%

commit v1 on v0

v1 whole, which is shorter than its diff:
```python
import functools

import jax
import jax.numpy as jnp
from jax import lax
from jax.experimental import pallas as pl
from jax.experimental.pallas import tpu as pltpu
from jax.sharding import PartitionSpec as P

MESH = pl.DeviceIdType.MESH
F32 = jnp.float32
BF16 = jnp.bfloat16
SIDE = 4
ZS = 8
GROUP = SIDE * SIDE
ROWS = 32
TOK = GROUP * ROWS
WID = 512
HID = 1792
LANES = 128
CH = 2 * LANES
NR = HID // CH
STAGES = 5


def dot(a, b):
    return jnp.dot(a, b, preferred_element_type=F32)


def dot_nt(a, b):
    return lax.dot_general(a, b, (((1,), (1,)), ((), ())), preferred_element_type=F32)


def dot_tn(a, b):
    return lax.dot_general(a, b, (((0,), (0,)), ((), ())), preferred_element_type=F32)


def kernel(
    tokens, grad_out, gate_w, up_w, down_w, gate_m, up_m, down_m,
    layer_out, grad_tokens, grad_gate, grad_up, grad_down,
    ab, tok_t, gw, uw, dw, part, own, recv1, mid, mid_own, recv2, full,
    out_g, out_u, out_d, acc, xbuf, zsend, zown, zrecv,
    load_sem, w_sem, a_send, a_recv, s_send, s_recv,
    send1, got1, send2, got2, send3, got3, send4, got4, out_sem,
    x_send, x_recv, z_send, z_recv,
):
    i = lax.axis_index("inb")
    o = lax.axis_index("outb")
    x, y = i // SIDE, lax.rem(i, SIDE)
    z, c = o // 2, lax.rem(o, 2)
    sib = 1 - c

    def at_x(k):
        return (lax.rem(x + k, SIDE) * SIDE + y, o)

    def at_y(k):
        return (x * SIDE + lax.rem(y + k, SIDE), o)

    def at_z(k):
        return (i, lax.rem(z + k, ZS) * 2 + c)

    sibling = (i, z * 2 + sib)

    def remote(src, dst, s, r, device):
        return pltpu.make_async_remote_copy(
            src_ref=src, dst_ref=dst, send_sem=s, recv_sem=r,
            device_id=device, device_id_type=MESH,
        )

    def drain(ref, sem):
        pltpu.make_async_copy(ref, ref, sem).wait()

    mine = c * ZS + z
    first = [
        pltpu.make_async_copy(tokens, ab.at[mine, 0], load_sem.at[0]),
        pltpu.make_async_copy(grad_out, ab.at[mine, 1], load_sem.at[1]),
    ]
    for copy in first:
        copy.start()
    weights = []
    for r in range(NR):
        cols = pl.ds(r * CH, CH)
        weights.append(pltpu.make_async_copy(gate_w.at[:, cols], gw.at[r], w_sem.at[0, r]))
        weights.append(pltpu.make_async_copy(up_w.at[:, cols], uw.at[r], w_sem.at[1, r]))
        weights.append(pltpu.make_async_copy(down_w.at[cols, :], dw.at[r], w_sem.at[2, r]))
    for copy in weights:
        copy.start()

    barrier = pltpu.get_barrier_semaphore()
    for k in range(1, SIDE):
        pl.semaphore_signal(barrier, inc=1, device_id=at_x(k), device_id_type=MESH)
        pl.semaphore_signal(barrier, inc=1, device_id=at_y(k), device_id_type=MESH)
    for k in range(1, ZS):
        pl.semaphore_signal(barrier, inc=1, device_id=at_z(k), device_id_type=MESH)
    pl.semaphore_signal(barrier, inc=1, device_id=sibling, device_id_type=MESH)
    pl.semaphore_wait(barrier, 2 * (SIDE - 1) + ZS - 1 + 1)

    for copy in first:
        copy.wait()
    own_block = ab.at[mine]
    order = (1, 7, 2, 6, 3, 5, 4)
    z_copies = [remote(own_block, own_block, a_send.at[k - 1], a_recv.at[k - 1], at_z(k)) for k in order]
    for copy in z_copies:
        copy.start()
    to_sib = [remote(own_block, own_block, s_send.at[0], s_recv, sibling)]
    to_sib[0].start()

    for copy in weights:
        copy.wait()
    for r in range(NR):
        for a in range(WID // LANES):
            for b in range(2):
                rows, cols = pl.ds(a * LANES, LANES), pl.ds(b * LANES, LANES)
                for w, m in ((gw, gate_m), (uw, up_m)):
                    keep = jnp.full((LANES, LANES), m[a, 2 * r + b].astype(F32), F32)
                    w[r, rows, cols] = w[r, rows, cols] * keep.astype(BF16)
                keep = jnp.full((LANES, LANES), down_m[2 * r + b, a].astype(F32), F32)
                dw[r, cols, rows] = dw[r, cols, rows] * keep.astype(BF16)

    for n, k in enumerate(order):
        block = ab.at[c * ZS + lax.rem(z + ZS - k, ZS)]
        remote(block, block, a_send.at[k - 1], a_recv.at[k - 1], at_z(k)).wait_recv()
        copy = remote(block, block, s_send.at[n + 1], s_recv, sibling)
        copy.start()
        to_sib.append(copy)
    drain(ab.at[pl.ds(sib * ZS, ZS)], s_recv)

    acc[...] = jnp.zeros_like(acc)

    def places(h):
        return (at_x, at_y, x, y) if h == 0 else (at_y, at_x, y, x)

    def partial_sums(r):
        tok = ab[:, 0].reshape(TOK, WID)
        cot = ab[:, 1].reshape(TOK, WID)
        slot = lax.rem(r, 2)
        for n in range(3):
            if n == 0:
                value = dot(tok, gw[r])
            elif n == 1:
                value = dot(tok, uw[r])
            else:
                value = dot_nt(cot, dw[r])
            for h in range(2):
                piece = value[:, h * LANES:(h + 1) * LANES].reshape(GROUP, ROWS, LANES)
                own[slot, h, :, n] = piece
                part[r, h, :, n] = piece.astype(BF16)
        for h in range(2):
            at1, _, p1, _ = places(h)
            for k in range(1, SIDE):
                to = lax.rem(p1 + k, SIDE)
                remote(
                    part.at[r, h, pl.ds(to * SIDE, SIDE)], recv1.at[r, h, k - 1],
                    send1.at[r, h], got1.at[r, h], at1(k),
                ).start()

    def second(r):
        slot = lax.rem(r, 2)
        for h in range(2):
            _, at2, p1, p2 = places(h)
            drain(recv1.at[r, h], got1.at[r, h])
            total = own[slot, h, pl.ds(p1 * SIDE, SIDE)]
            for k in range(SIDE - 1):
                total = total + recv1[r, h, k].astype(F32)
            mid_own[slot, h] = total
            mid[r, h] = total.astype(BF16)
            for k in range(1, SIDE):
                to = lax.rem(p2 + k, SIDE)
                remote(
                    mid.at[r, h, to], recv2.at[r, h, k - 1],
                    send2.at[r, h], got2.at[r, h], at2(k),
                ).start()

    def activations(r):
        slot = lax.rem(r, 2)
        for h in range(2):
            _, at2, p1, p2 = places(h)
            drain(recv2.at[r, h], got2.at[r, h])
            total = mid_own[slot, h, p2]
            for k in range(SIDE - 1):
                total = total + recv2[r, h, k].astype(F32)
            gate, up, hidden_grad = total[0], total[1], total[2]
            sig = jax.nn.sigmoid(gate)
            act = gate * sig
            at = p1 * SIDE + p2
            full[r, h, at, 0] = (act * up).astype(BF16)
            full[r, h, at, 1] = (hidden_grad * up * sig * (1.0 + gate * (1.0 - sig))).astype(BF16)
            full[r, h, at, 2] = (hidden_grad * act).astype(BF16)
            for k in range(1, SIDE):
                block = full.at[r, h, at]
                remote(block, block, send3.at[r, h], got3.at[r, h], at2(k)).start()

    def spread(r):
        for h in range(2):
            at1, _, p1, _ = places(h)
            drain(recv2.at[r, h], got3.at[r, h])
            for k in range(1, SIDE):
                block = full.at[r, h, pl.ds(p1 * SIDE, SIDE)]
                remote(block, block, send4.at[r, h], got4.at[r, h], at1(k)).start()

    def finish(r):
        drain(recv1.at[r, 0], got4.at[r, 0])
        drain(recv1.at[r, 1], got4.at[r, 1])

        def whole(n):
            return jnp.concatenate(
                [full[r, h, :, n].reshape(TOK, LANES) for h in range(2)], axis=1
            )

        hidden, gate_grad, up_grad = whole(0), whole(1), whole(2)
        half = TOK // 2
        value = dot(hidden, dw[r])
        acc[0, 0] += value[:half]
        acc[1, 0] += value[half:]
        value = dot_nt(gate_grad, gw[r]) + dot_nt(up_grad, uw[r])
        acc[0, 1] += value[:half]
        acc[1, 1] += value[half:]
        cot = ab[:, 1].reshape(TOK, WID)
        for out, left, m in ((out_g, gate_grad, gate_m), (out_u, up_grad, up_m)):
            value = dot(tok_t[...], left)
            for a in range(WID // LANES):
                for b in range(2):
                    rows, cols = slice(a * LANES, (a + 1) * LANES), slice(b * LANES, (b + 1) * LANES)
                    keep = m[a, 2 * r + b].astype(F32)
                    out[r, rows, cols] = (value[rows, cols] * keep).astype(BF16)
        value = dot_tn(hidden, cot)
        for a in range(WID // LANES):
            for b in range(2):
                rows, cols = slice(a * LANES, (a + 1) * LANES), slice(b * LANES, (b + 1) * LANES)
                keep = down_m[2 * r + b, a].astype(F32)
                out_d[r, cols, rows] = (value[cols, rows] * keep).astype(BF16)
        for copy in outs(r):
            copy.start()

    def outs(r):
        cols = pl.ds(pl.multiple_of(r * CH, CH), CH)
        return [
            pltpu.make_async_copy(out_g.at[r], grad_gate.at[:, cols], out_sem.at[0, r]),
            pltpu.make_async_copy(out_u.at[r], grad_up.at[:, cols], out_sem.at[1, r]),
            pltpu.make_async_copy(out_d.at[r], grad_down.at[cols, :], out_sem.at[2, r]),
        ]

    @pl.loop(0, NR + STAGES - 1)
    def _(t):
        for stage, work in enumerate((partial_sums, second, activations, spread, finish)):
            @pl.when(jnp.logical_and(t >= stage, t < NR + stage))
            def _():
                work(t - stage)

            if stage == 0:
                @pl.when(t == 1)
                def _():
                    tok_t[...] = ab[:, 0].reshape(TOK, WID).T

    copy = remote(acc.at[sib], xbuf, x_send, x_recv, sibling)
    copy.start()
    copy.wait_recv()
    for k in list(order) + [0]:
        to = lax.rem(z + k, ZS)
        rows = pl.ds(pl.multiple_of(to * ROWS, ROWS), ROWS)
        for a in range(2):
            value = acc[c, a, rows] + xbuf[a, rows]
            if k == 0:
                zown[a] = value
            else:
                zsend[k - 1, a] = value.astype(BF16)
        if k:
            remote(zsend.at[k - 1], zrecv.at[k - 1], z_send, z_recv, at_z(k)).start()
    drain(zrecv, z_recv)
    for a, out in enumerate((layer_out, grad_tokens)):
        value = zown[a]
        for k in range(ZS - 1):
            value = value + zrecv[k, a].astype(F32)
        out[...] = value.astype(BF16)

    drain(zrecv, z_send)
    copy.wait_send()
    for copy in z_copies:
        copy.wait_send()
    for copy in to_sib:
        copy.wait_send()

    @pl.loop(0, NR)
    def _(r):
        for h in range(2):
            drain(recv1.at[r, h], send1.at[r, h])
            drain(recv2.at[r, h], send2.at[r, h])
            drain(recv2.at[r, h], send3.at[r, h])
            drain(recv1.at[r, h], send4.at[r, h])
        for copy in outs(r):
            copy.wait()


def local(tokens, grad_out, gate_weight, up_weight, down_weight, gate_mask, up_mask, down_mask):
    any_spec = pl.BlockSpec(memory_space=pl.ANY)
    vmem = pl.BlockSpec(memory_space=pltpu.VMEM)
    smem = pl.BlockSpec(memory_space=pltpu.SMEM)
    dma = pltpu.SemaphoreType.DMA
    block = (3, ROWS, LANES)
    return pl.pallas_call(
        kernel,
        name="sparse_swiglu_step",
        out_shape=[
            jax.ShapeDtypeStruct((ROWS, WID), BF16),
            jax.ShapeDtypeStruct((ROWS, WID), BF16),
            jax.ShapeDtypeStruct((WID, HID), BF16),
            jax.ShapeDtypeStruct((WID, HID), BF16),
            jax.ShapeDtypeStruct((HID, WID), BF16),
        ],
        in_specs=[any_spec] * 5 + [smem] * 3,
        out_specs=[vmem, vmem, any_spec, any_spec, any_spec],
        scratch_shapes=[
            pltpu.VMEM((2 * ZS, 2, ROWS, WID), BF16),
            pltpu.VMEM((WID, TOK), BF16),
            pltpu.VMEM((NR, WID, CH), BF16),
            pltpu.VMEM((NR, WID, CH), BF16),
            pltpu.VMEM((NR, CH, WID), BF16),
            pltpu.VMEM((NR, 2, GROUP) + block, BF16),
            pltpu.VMEM((2, 2, GROUP) + block, F32),
            pltpu.VMEM((NR, 2, SIDE - 1, SIDE) + block, BF16),
            pltpu.VMEM((NR, 2, SIDE) + block, BF16),
            pltpu.VMEM((2, 2, SIDE) + block, F32),
            pltpu.VMEM((NR, 2, SIDE - 1) + block, BF16),
            pltpu.VMEM((NR, 2, GROUP) + block, BF16),
            pltpu.VMEM((NR, WID, CH), BF16),
            pltpu.VMEM((NR, WID, CH), BF16),
            pltpu.VMEM((NR, CH, WID), BF16),
            pltpu.VMEM((2, 2, TOK // 2, WID), F32),
            pltpu.VMEM((2, TOK // 2, WID), F32),
            pltpu.VMEM((ZS - 1, 2, ROWS, WID), BF16),
            pltpu.VMEM((2, ROWS, WID), F32),
            pltpu.VMEM((ZS - 1, 2, ROWS, WID), BF16),
            dma((2,)),
            dma((3, NR)),
            dma((ZS - 1,)), dma((ZS - 1,)),
            dma((ZS,)), dma,
            dma((NR, 2)), dma((NR, 2)),
            dma((NR, 2)), dma((NR, 2)),
            dma((NR, 2)), dma((NR, 2)),
            dma((NR, 2)), dma((NR, 2)),
            dma((3, NR)),
            dma, dma, dma, dma,
        ],
        compiler_params=pltpu.CompilerParams(
            collective_id=0, has_side_effects=True, vmem_limit_bytes=56 << 20
        ),
    )(tokens, grad_out, gate_weight, up_weight, down_weight, gate_mask, up_mask, down_mask)


def solution(mesh):
    wide, tall = P("inb", "outb"), P("outb", "inb")
    return jax.shard_map(
        local,
        mesh=mesh,
        in_specs=(tall, tall, wide, wide, tall, wide, wide, tall),
        out_specs=(tall, tall, wide, wide, tall),
        check_vma=False,
    )
```

time: 566 us -> 134 us (0.24)
  waiting for transfers between devices: 454 us -> 0 us
  Pallas kernels: 0 us -> 122 us
  blocking collectives: 39 us -> 0 us
  matrix products: 27 us -> 0 us
  between operations: 14.2 us -> 0.64 us
  local copies, waits for them, and re-layouts: 23.1 us -> 10.5 us
  other arithmetic: 5.73 us -> 0 us
    reduce_scatter x5 -> x0, waiting for transfers between devices: 311 us -> none  [the longest x1 84.5 us: local(): lax.psum_scatter(hidden_part, 'inb', scatter_dimension=1, tiled=True)]
    all_gather x3 -> x0, waiting for transfers between devices: 141 us -> none  [the longest x1 48.3 us: local(): lax.all_gather(gate_grad, 'inb', axis=1, tiled=True)]
    pallas_call x0 -> x1, Pallas kernels: none -> 122 us  [local(): pl.pallas_call(kernel, name='sparse_swiglu_step', out_shape=[jax.ShapeDty...]
    all_gather x2 -> x0, blocking collectives: 39 us -> none  [the longest x1 23 us: local(): tokens_all = lax.all_gather(tokens, 'outb', axis=0, tiled=True)]
    dot_general x9 -> x0, matrix products: 27 us -> none  [the longest x3 12.2 us: times_transpose(): lax.dot_general(left, right, (((1,), (1,)), ((), ())), preferred_element_...]
    unnamed x28 -> x10, local copies, waits for them, and re-layouts: 19.3 us -> 10.5 us
    convert_element_type x6 -> x0, other arithmetic: 5.73 us -> none  [the longest x1 2.04 us: swiglu_grad(): up_grad = (hidden_grad * gate * sigmoid_gate).astype(jnp.bfloat16)]
  transfers between devices with their start and end apart: 8 -> 0, of which waited for: 8 -> 0; matrix products, arithmetic and copies ran while one was open for 7% -> 0% of each run, Pallas kernels for 0% -> 0%
where the time goes in v1:
time: 134 us
  Pallas kernels  122 us (91%)
  local copies, waits for them, and re-layouts  10.5 us (8%)
    pallas_call x1, Pallas kernels, local(): pl.pallas_call(kernel, name='sparse_swiglu_step', out_shape=[jax.ShapeDty...  122 us
    unnamed x10, local copies, waits for them, and re-layouts  10.5 us

profile of v1, /device:TPU:1, one launch (start us, length us, event | category | flops | bytes accessed | tf_op | source)
XLA Modules:
  0.0 133.6 jit_solution(17135274248441403285)
XLA Ops:
  0.6 1.4 %copy.13.down_m = s32[14,4]{1,0:T(8,128)} copy(s32[14,4]{0,1:T(4,128)} %param.15) | data formatting | bytes 448 | tf_op args[7]
  2.0 122.5 %sparse_swiglu_step.1 = (bf16[32,512]{1,0:T(8,128)(2,1)}, bf16[32,512]{1,0:T(8,128)(2,1)}, bf16[512,1792]{1,0:T(8,128)(2,1)}, bf16[512,1792]{1,0:T(8,128)(2,1)}, bf16[1792,512]{1,0:T(8,128)(2,1)}) custom-call(bf16[32,512]{1,0:T(8,128)(2,1)} %tokens.1, bf16[32,512]{1,0:T(8,128)(2,1)} %grad_out.1, bf16[512,1792]{1,0:T(8,128)(2,1)} %gate_w.1, ...), custom_call_target="tpu_custom_call" | custom-call | tf_op jit(solution)/shard_map/sparse_swiglu_step/pallas_call | solution.py:300
  124.5 1.4 %copy.19 = bf16[32,512]{1,0:T(8,128)(2,1)} copy(bf16[32,512]{1,0:T(8,128)(2,1)} %get-tuple-element.10) | data formatting | bytes 65536
  125.8 1.4 %copy.20 = bf16[32,512]{1,0:T(8,128)(2,1)} copy(bf16[32,512]{1,0:T(8,128)(2,1)} %get-tuple-element.11) | data formatting | bytes 65536
  127.2 0.0 copy-start.1
  127.2 3.0 %copy.21 = bf16[512,1792]{1,0:T(8,128)(2,1)} copy(bf16[512,1792]{1,0:T(8,128)(2,1)} %get-tuple-element.12) | data formatting | bytes 3670016
  130.2 0.0 copy-done.1
  130.2 0.0 copy-start
  130.2 1.2 copy.22
  131.4 0.9 copy-done
  132.4 1.2 copy.23
Async XLA Ops:
  127.2 3.0 %copy-start.1 = (bf16[512,1792]{1,0:T(8,128)(2,1)S(1)}, bf16[512,1792]{1,0:T(8,128)(2,1)}, u32[]{:S(2)}) copy-start(bf16[512,1792]{1,0:T(8,128)(2,1)} %get-tuple-element.13) | copy-start | bytes 5505028
  130.2 2.2 %copy-start = (bf16[1792,512]{1,0:T(8,128)(2,1)S(1)}, bf16[1792,512]{1,0:T(8,128)(2,1)}, u32[]{:S(2)}) copy-start(bf16[1792,512]{1,0:T(8,128)(2,1)} %get-tuple-element.14) | copy-start | bytes 5505028

commit v2 on v1

v2 whole, which is shorter than its diff:
```python
import functools

import jax
import jax.numpy as jnp
from jax import lax
from jax.experimental import pallas as pl
from jax.experimental.pallas import tpu as pltpu
from jax.sharding import PartitionSpec as P

MESH = pl.DeviceIdType.MESH
F32 = jnp.float32
BF16 = jnp.bfloat16
SIDE = 4
ZS = 8
GROUP = SIDE * SIDE
ROWS = 32
HALF = ROWS // 2
TOK = GROUP * HALF
WID = 512
HID = 1792
LANES = 128
CH = 2 * LANES
NR = HID // CH
NQ = 2 * NR
LAG = 2
KEEP = LAG + 1
LAST = NQ + 4 * LAG


def dot(a, b):
    return jnp.dot(a, b, preferred_element_type=F32)


def dot_nt(a, b):
    return lax.dot_general(a, b, (((1,), (1,)), ((), ())), preferred_element_type=F32)


def dot_tn(a, b):
    return lax.dot_general(a, b, (((0,), (0,)), ((), ())), preferred_element_type=F32)


def kernel(
    tokens, grad_out, gate_w, up_w, down_w, gate_mask, up_mask, down_mask,
    layer_out, grad_tokens, grad_gate, grad_up, grad_down,
    gate_m, up_m, down_m, ab, tok_t, gw, uw, dw, part, own, recv1, mid, mid_own, recv2, full,
    out_g, out_u, out_d, acc, xbuf, zsend, zown, zrecv,
    load_sem, m_sem, w_sem, a_send, a_recv, s_send, s_recv,
    send1, got1, send2, got2, send3, got3, send4, got4, out_sem,
    x_send, x_recv, z_send, z_recv,
):
    i = lax.axis_index("inb")
    o = lax.axis_index("outb")
    x, y = i // SIDE, lax.rem(i, SIDE)
    z, c = o // 2, lax.rem(o, 2)
    sib = 1 - c

    def at_x(k):
        return (lax.rem(x + k, SIDE) * SIDE + y, o)

    def at_y(k):
        return (x * SIDE + lax.rem(y + k, SIDE), o)

    def at_z(k):
        return (i, lax.rem(z + k, ZS) * 2 + c)

    sibling = (i, z * 2 + sib)

    def remote(src, dst, s, r, device):
        return pltpu.make_async_remote_copy(
            src_ref=src, dst_ref=dst, send_sem=s, recv_sem=r,
            device_id=device, device_id_type=MESH,
        )

    def drain(ref, sem):
        pltpu.make_async_copy(ref, ref, sem).wait()

    mine = c * ZS + z
    first = []
    for th in range(2):
        rows = pl.ds(th * HALF, HALF)
        first.append(pltpu.make_async_copy(tokens.at[rows], ab.at[th, mine, 0], load_sem.at[th, 0]))
        first.append(pltpu.make_async_copy(grad_out.at[rows], ab.at[th, mine, 1], load_sem.at[th, 1]))
    for copy in first:
        copy.start()
    weights = [
        pltpu.make_async_copy(gate_mask, gate_m, m_sem.at[0]),
        pltpu.make_async_copy(up_mask, up_m, m_sem.at[1]),
        pltpu.make_async_copy(down_mask, down_m, m_sem.at[2]),
    ]
    for r in range(NR):
        cols = pl.ds(r * CH, CH)
        weights.append(pltpu.make_async_copy(gate_w.at[:, cols], gw.at[r], w_sem.at[0, r]))
        weights.append(pltpu.make_async_copy(up_w.at[:, cols], uw.at[r], w_sem.at[1, r]))
        weights.append(pltpu.make_async_copy(down_w.at[cols, :], dw.at[r], w_sem.at[2, r]))
    for copy in weights:
        copy.start()

    barrier = pltpu.get_barrier_semaphore()
    for k in range(1, SIDE):
        pl.semaphore_signal(barrier, inc=1, device_id=at_x(k), device_id_type=MESH)
        pl.semaphore_signal(barrier, inc=1, device_id=at_y(k), device_id_type=MESH)
    for k in range(1, ZS):
        pl.semaphore_signal(barrier, inc=1, device_id=at_z(k), device_id_type=MESH)
    pl.semaphore_signal(barrier, inc=1, device_id=sibling, device_id_type=MESH)
    pl.semaphore_wait(barrier, 2 * (SIDE - 1) + ZS - 1 + 1)

    order = (4, 3, 5, 2, 6, 1, 7)
    near = (1, 7, 2, 6, 3, 5, 4)

    def z_copy(th, k):
        block = ab.at[th, mine]
        return remote(block, block, a_send.at[th, k - 1], a_recv.at[th, k - 1], at_z(k))

    def to_sibling(th, k):
        block = ab.at[th, c * ZS + lax.rem(z + ZS - k, ZS)]
        return remote(block, block, s_send.at[th, k], s_recv.at[th], sibling)

    def gather_start(th):
        for k in order:
            z_copy(th, k).start()
        to_sibling(th, 0).start()

    def gather_relay(th):
        for k in near:
            z_copy(th, k).wait_recv()
            to_sibling(th, k).start()

    def gather_end(th):
        drain(ab.at[th, pl.ds(sib * ZS, ZS)], s_recv.at[th])

    for copy in first:
        copy.wait()
    gather_start(0)

    acc[...] = jnp.zeros_like(acc)
    for copy in weights:
        copy.wait()
    for r in range(NR):
        for a in range(WID // LANES):
            for b in range(2):
                rows, cols = pl.ds(a * LANES, LANES), pl.ds(b * LANES, LANES)
                for w, m in ((gw, gate_m), (uw, up_m)):
                    keep = jnp.full((LANES, LANES), m[a, 2 * r + b].astype(F32), F32)
                    w[r, rows, cols] = w[r, rows, cols] * keep.astype(BF16)
                keep = jnp.full((LANES, LANES), down_m[a, 2 * r + b].astype(F32), F32)
                dw[r, cols, rows] = dw[r, cols, rows] * keep.astype(BF16)

    gather_relay(0)
    gather_end(0)
    gather_start(1)

    def places(h):
        return (at_x, at_y, x, y) if h == 0 else (at_y, at_x, y, x)

    def half_of(q):
        th = q // NR
        return th, q - th * NR

    def partial_sums(q):
        th, r = half_of(q)
        tok = ab[th, :, 0].reshape(TOK, WID)
        cot = ab[th, :, 1].reshape(TOK, WID)
        slot = lax.rem(q, KEEP)
        for n in range(3):
            if n == 0:
                value = dot(tok, gw[r])
            elif n == 1:
                value = dot(tok, uw[r])
            else:
                value = dot_nt(cot, dw[r])
            for h in range(2):
                piece = value[:, h * LANES:(h + 1) * LANES].reshape(GROUP, HALF, LANES)
                own[slot, h, :, n] = piece
                part[q, h, :, n] = piece.astype(BF16)
        for h in range(2):
            at1, _, p1, _ = places(h)
            for k in range(1, SIDE):
                to = lax.rem(p1 + k, SIDE)
                remote(
                    part.at[q, h, pl.ds(to * SIDE, SIDE)], recv1.at[q, h, k - 1],
                    send1.at[q, h], got1.at[q, h], at1(k),
                ).start()

    def second(q):
        slot = lax.rem(q, KEEP)
        for h in range(2):
            _, at2, p1, p2 = places(h)
            drain(recv1.at[q, h], got1.at[q, h])
            total = own[slot, h, pl.ds(p1 * SIDE, SIDE)]
            for k in range(SIDE - 1):
                total = total + recv1[q, h, k].astype(F32)
            mid_own[slot, h] = total
            mid[q, h] = total.astype(BF16)
            for k in range(1, SIDE):
                to = lax.rem(p2 + k, SIDE)
                remote(
                    mid.at[q, h, to], recv2.at[q, h, k - 1],
                    send2.at[q, h], got2.at[q, h], at2(k),
                ).start()

    def activations(q):
        slot = lax.rem(q, KEEP)
        for h in range(2):
            _, at2, p1, p2 = places(h)
            drain(recv2.at[q, h], got2.at[q, h])
            total = mid_own[slot, h, p2]
            for k in range(SIDE - 1):
                total = total + recv2[q, h, k].astype(F32)
            gate, up, hidden_grad = total[0], total[1], total[2]
            sig = jax.nn.sigmoid(gate)
            act = gate * sig
            at = p1 * SIDE + p2
            full[q, h, at, 0] = (act * up).astype(BF16)
            full[q, h, at, 1] = (hidden_grad * up * sig * (1.0 + gate * (1.0 - sig))).astype(BF16)
            full[q, h, at, 2] = (hidden_grad * act).astype(BF16)
            for k in range(1, SIDE):
                block = full.at[q, h, at]
                remote(block, block, send3.at[q, h], got3.at[q, h], at2(k)).start()

    def spread(q):
        for h in range(2):
            at1, _, p1, _ = places(h)
            drain(recv2.at[q, h], got3.at[q, h])
            for k in range(1, SIDE):
                block = full.at[q, h, pl.ds(p1 * SIDE, SIDE)]
                remote(block, block, send4.at[q, h], got4.at[q, h], at1(k)).start()

    def whole(q, n):
        return jnp.concatenate(
            [full[q, h, :, n].reshape(TOK, LANES) for h in range(2)], axis=1
        )

    def finish(q):
        th, r = half_of(q)
        drain(recv1.at[q, 0], got4.at[q, 0])
        drain(recv1.at[q, 1], got4.at[q, 1])
        hidden, gate_grad, up_grad = whole(q, 0), whole(q, 1), whole(q, 2)
        half = TOK // 2
        value = dot(hidden, dw[r])
        acc[th, 0, 0] += value[:half]
        acc[th, 1, 0] += value[half:]
        value = dot_nt(gate_grad, gw[r]) + dot_nt(up_grad, uw[r])
        acc[th, 0, 1] += value[:half]
        acc[th, 1, 1] += value[half:]

        @pl.when(r == NR - 1)
        def _():
            cores_start(th)

    def weight_grads(r):
        for out, n, m in ((out_g, 1, gate_m), (out_u, 2, up_m)):
            value = dot(tok_t[0], whole(r, n)) + dot(tok_t[1], whole(r + NR, n))
            for a in range(WID // LANES):
                for b in range(2):
                    rows, cols = slice(a * LANES, (a + 1) * LANES), slice(b * LANES, (b + 1) * LANES)
                    keep = m[a, 2 * r + b].astype(F32)
                    out[r, rows, cols] = (value[rows, cols] * keep).astype(BF16)
        value = dot_tn(whole(r, 0), ab[0, :, 1].reshape(TOK, WID))
        value = value + dot_tn(whole(r + NR, 0), ab[1, :, 1].reshape(TOK, WID))
        for a in range(WID // LANES):
            for b in range(2):
                rows, cols = slice(a * LANES, (a + 1) * LANES), slice(b * LANES, (b + 1) * LANES)
                keep = down_m[a, 2 * r + b].astype(F32)
                out_d[r, cols, rows] = (value[cols, rows] * keep).astype(BF16)
        for copy in outs(r):
            copy.start()

    def outs(r):
        cols = pl.ds(pl.multiple_of(r * CH, CH), CH)
        return [
            pltpu.make_async_copy(out_g.at[r], grad_gate.at[:, cols], out_sem.at[0, r]),
            pltpu.make_async_copy(out_u.at[r], grad_up.at[:, cols], out_sem.at[1, r]),
            pltpu.make_async_copy(out_d.at[r], grad_down.at[cols, :], out_sem.at[2, r]),
        ]

    def cores_copy(th):
        return remote(acc.at[th, sib], xbuf.at[th], x_send.at[th], x_recv.at[th], sibling)

    def cores_start(th):
        cores_copy(th).start()

    def z_start(th):
        cores_copy(th).wait_recv()
        for k in order + (0,):
            to = lax.rem(z + k, ZS)
            rows = pl.ds(pl.multiple_of(to * HALF, HALF), HALF)
            for a in range(2):
                value = acc[th, c, a, rows] + xbuf[th, a, rows]
                if k == 0:
                    zown[th, a] = value
                else:
                    zsend[th, k - 1, a] = value.astype(BF16)
            if k:
                remote(
                    zsend.at[th, k - 1], zrecv.at[th, k - 1], z_send.at[th], z_recv.at[th], at_z(k)
                ).start()

    def z_end(th):
        drain(zrecv.at[th], z_recv.at[th])
        for a, out in enumerate((layer_out, grad_tokens)):
            value = zown[th, a]
            for k in range(ZS - 1):
                value = value + zrecv[th, k, a].astype(F32)
            out[pl.ds(th * HALF, HALF)] = value.astype(BF16)

    @pl.loop(0, LAST)
    def _(t):
        def stage(s, work):
            @pl.when(jnp.logical_and(t >= s * LAG, t < NQ + s * LAG))
            def _():
                work(t - s * LAG)

        stage(1, second)
        stage(2, activations)
        stage(3, spread)

        @pl.when(t == NR - 1)
        def _():
            gather_relay(1)

        @pl.when(t == NR)
        def _():
            gather_end(1)

        stage(0, partial_sums)

        @pl.when(t == NR + 1)
        def _():
            for th in range(2):
                tok_t[th] = ab[th, :, 0].reshape(TOK, WID).T

        stage(4, finish)

        @pl.when(t >= NR + 4 * LAG)
        def _():
            weight_grads(t - NR - 4 * LAG)

        @pl.when(t == NR + 4 * LAG)
        def _():
            z_start(0)

    z_start(1)
    z_end(0)
    z_end(1)

    for th in range(2):
        drain(zrecv.at[th], z_send.at[th])
        cores_copy(th).wait_send()
        for k in range(ZS):
            if k:
                z_copy(th, k).wait_send()
            to_sibling(th, k).wait_send()

    @pl.loop(0, NQ)
    def _(q):
        for h in range(2):
            drain(recv1.at[q, h], send1.at[q, h])
            drain(recv2.at[q, h], send2.at[q, h])
            drain(recv2.at[q, h], send3.at[q, h])
            drain(recv1.at[q, h], send4.at[q, h])

    @pl.loop(0, NR)
    def _(r):
        for copy in outs(r):
            copy.wait()


def hand_over(*refs):
    n = len(refs) // 2
    sem = refs[-1]
    copies = [pltpu.make_async_copy(refs[j], refs[n + j], sem.at[j]) for j in range(n)]
    for copy in copies:
        copy.start()
    for copy in copies:
        copy.wait()


def local(tokens, grad_out, gate_weight, up_weight, down_weight, gate_mask, up_mask, down_mask):
    any_spec = pl.BlockSpec(memory_space=pl.ANY)
    vmem = pl.BlockSpec(memory_space=pltpu.VMEM)
    hbm = pl.BlockSpec(memory_space=pltpu.HBM)
    dma = pltpu.SemaphoreType.DMA
    block = (3, HALF, LANES)
    shapes = [
        jax.ShapeDtypeStruct((ROWS, WID), BF16),
        jax.ShapeDtypeStruct((ROWS, WID), BF16),
        jax.ShapeDtypeStruct((WID, HID), BF16),
        jax.ShapeDtypeStruct((WID, HID), BF16),
        jax.ShapeDtypeStruct((HID, WID), BF16),
    ]
    results = pl.pallas_call(
        kernel,
        name="sparse_swiglu_step",
        out_shape=shapes,
        in_specs=[hbm] * 8,
        out_specs=[vmem, vmem, any_spec, any_spec, any_spec],
        scratch_shapes=[
            pltpu.SMEM((WID // LANES, HID // LANES), jnp.int32),
            pltpu.SMEM((WID // LANES, HID // LANES), jnp.int32),
            pltpu.SMEM((WID // LANES, HID // LANES), jnp.int32),
            pltpu.VMEM((2, 2 * ZS, 2, HALF, WID), BF16),
            pltpu.VMEM((2, WID, TOK), BF16),
            pltpu.VMEM((NR, WID, CH), BF16),
            pltpu.VMEM((NR, WID, CH), BF16),
            pltpu.VMEM((NR, CH, WID), BF16),
            pltpu.VMEM((NQ, 2, GROUP) + block, BF16),
            pltpu.VMEM((KEEP, 2, GROUP) + block, F32),
            pltpu.VMEM((NQ, 2, SIDE - 1, SIDE) + block, BF16),
            pltpu.VMEM((NQ, 2, SIDE) + block, BF16),
            pltpu.VMEM((KEEP, 2, SIDE) + block, F32),
            pltpu.VMEM((NQ, 2, SIDE - 1) + block, BF16),
            pltpu.VMEM((NQ, 2, GROUP) + block, BF16),
            pltpu.VMEM((NR, WID, CH), BF16),
            pltpu.VMEM((NR, WID, CH), BF16),
            pltpu.VMEM((NR, CH, WID), BF16),
            pltpu.VMEM((2, 2, 2, TOK // 2, WID), F32),
            pltpu.VMEM((2, 2, TOK // 2, WID), F32),
            pltpu.VMEM((2, ZS - 1, 2, HALF, WID), BF16),
            pltpu.VMEM((2, 2, HALF, WID), F32),
            pltpu.VMEM((2, ZS - 1, 2, HALF, WID), BF16),
            dma((2, 2)),
            dma((3,)),
            dma((3, NR)),
            dma((2, ZS - 1)), dma((2, ZS - 1)),
            dma((2, ZS)), dma((2,)),
            dma((NQ, 2)), dma((NQ, 2)),
            dma((NQ, 2)), dma((NQ, 2)),
            dma((NQ, 2)), dma((NQ, 2)),
            dma((NQ, 2)), dma((NQ, 2)),
            dma((3, NR)),
            dma((2,)), dma((2,)), dma((2,)), dma((2,)),
        ],
        compiler_params=pltpu.CompilerParams(
            collective_id=0, has_side_effects=True, vmem_limit_bytes=48 << 20
        ),
    )(*(
        pltpu.with_memory_space_constraint(value, pltpu.HBM)
        for value in (
            tokens, grad_out, gate_weight, up_weight, down_weight, gate_mask, up_mask, down_mask.T
        )
    ))
    return pl.pallas_call(
        hand_over,
        name="hand_over",
        out_shape=shapes,
        in_specs=[any_spec] * 5,
        out_specs=[any_spec] * 5,
        scratch_shapes=[dma((5,))],
        compiler_params=pltpu.CompilerParams(vmem_limit_bytes=1 << 20),
    )(*results)


def solution(mesh):
    wide, tall = P("inb", "outb"), P("outb", "inb")
    return jax.shard_map(
        local,
        mesh=mesh,
        in_specs=(tall, tall, wide, wide, tall, wide, wide, tall),
        out_specs=(tall, tall, wide, wide, tall),
        check_vma=False,
    )
```

time: 134 us -> 113 us (0.84)
  local copies, waits for them, and re-layouts: 10.5 us -> 0 us
  Pallas kernels: 122 us -> 113 us
    unnamed x10 -> x0, local copies, waits for them, and re-layouts: 10.5 us -> none
    pallas_call x1 -> x2, Pallas kernels: 122 us -> 113 us  [the longest x1 110 us: local(): pl.pallas_call(kernel, name='sparse_swiglu_step', out_shape=shapes, in_sp...]
where the time goes in v2:
time: 113 us
  Pallas kernels  113 us (100%)
    pallas_call x1, Pallas kernels, local(): pl.pallas_call(kernel, name='sparse_swiglu_step', out_shape=shapes, in_sp...  110 us
    pallas_call x1, Pallas kernels, local(): pl.pallas_call(hand_over, name='hand_over', out_shape=shapes, in_specs=[a...  2.5 us

profile of v2, /device:TPU:1, one launch (start us, length us, event | category | flops | bytes accessed | tf_op | source)
XLA Modules:
  0.0 113.4 jit_solution(4117258240070742796)
XLA Ops:
  0.6 110.2 %sparse_swiglu_step.1 = (bf16[32,512]{1,0:T(8,128)(2,1)S(1)}, bf16[32,512]{1,0:T(8,128)(2,1)S(1)}, bf16[512,1792]{1,0:T(8,128)(2,1)S(1)}, bf16[512,1792]{1,0:T(8,128)(2,1)S(1)}, bf16[1792,512]{1,0:T(8,128)(2,1)S(1)}) custom-call(bf16[32,512]{1,0:T(8,128)(2,1)} %tokens.1, bf16[32,512]{1,0:T(8,128)(2,1)} %grad_out.1, bf16[512,1792]{1,0:T(8,128)(2,1)} %gate_w.1, ...), custom_call_target="tpu_custom_call" | custom-call | tf_op jit(solution)/shard_map/sparse_swiglu_step/pallas_call | solution.py:391
  110.9 2.5 %hand_over.1 = (bf16[32,512]{1,0:T(8,128)(2,1)}, bf16[32,512]{1,0:T(8,128)(2,1)}, bf16[512,1792]{1,0:T(8,128)(2,1)}, bf16[512,1792]{1,0:T(8,128)(2,1)}, bf16[1792,512]{1,0:T(8,128)(2,1)}) custom-call(bf16[32,512]{1,0:T(8,128)(2,1)S(1)} %get-tuple-element.10.refs_0_, bf16[32,512]{1,0:T(8,128)(2,1)S(1)} %get-tuple-element.11.refs_1_, ...), custom_call_target="tpu_custom_call" | custom-call | tf_op jit(solution)/shard_map/hand_over/pallas_call | solution.py:442

commit v3 on v2

--- a/solution.py
+++ b/solution.py
@@ -15,6 +15,7 @@
 GROUP = SIDE * SIDE
 ROWS = 32
 HALF = ROWS // 2
+PAIR = SIDE // 2
 TOK = GROUP * HALF
 WID = 512
 HID = 1792
@@ -24,7 +25,9 @@
 NQ = 2 * NR
 LAG = 2
 KEEP = LAG + 1
-LAST = NQ + 4 * LAG
+KEEP_OWN = 2 * LAG + 1
+STAGES = 7
+LAST = NQ + (STAGES - 1) * LAG
 
 
 def dot(a, b):
@@ -43,9 +46,9 @@
     tokens, grad_out, gate_w, up_w, down_w, gate_mask, up_mask, down_mask,
     layer_out, grad_tokens, grad_gate, grad_up, grad_down,
     gate_m, up_m, down_m, ab, tok_t, gw, uw, dw, part, own, recv1, mid, mid_own, recv2, full,
-    out_g, out_u, out_d, acc, xbuf, zsend, zown, zrecv,
+    chain, out_g, out_u, out_d, acc, xbuf, zown, zsend_0, zsend_1, zrecv_0, zrecv_1,
     load_sem, m_sem, w_sem, a_send, a_recv, s_send, s_recv,
-    send1, got1, send2, got2, send3, got3, send4, got4, out_sem,
+    send1, got0, got1, send2, got2, send3, got3, send4, got4, got5, out_sem,
     x_send, x_recv, z_send, z_recv,
 ):
     i = lax.axis_index("inb")
@@ -160,7 +163,7 @@
         th, r = half_of(q)
         tok = ab[th, :, 0].reshape(TOK, WID)
         cot = ab[th, :, 1].reshape(TOK, WID)
-        slot = lax.rem(q, KEEP)
+        slot = lax.rem(q, KEEP_OWN)
         for n in range(3):
             if n == 0:
                 value = dot(tok, gw[r])
@@ -174,23 +177,46 @@
                 part[q, h, :, n] = piece.astype(BF16)
         for h in range(2):
             at1, _, p1, _ = places(h)
-            for k in range(1, SIDE):
-                to = lax.rem(p1 + k, SIDE)
+            after, far, before = (lax.rem(p1 + k, SIDE) * SIDE for k in range(1, SIDE))
+            for start, slot_to, sem, k in (
+                (far, 0, got0, 1), (far + PAIR, 1, got0, 3),
+                (after + PAIR, 2, got1, 1), (before, 3, got1, 3),
+            ):
                 remote(
-                    part.at[q, h, pl.ds(to * SIDE, SIDE)], recv1.at[q, h, k - 1],
+                    part.at[q, h, pl.ds(start, PAIR)], recv1.at[q, h, slot_to],
+                    send1.at[q, h], sem.at[q, h], at1(k),
+                ).start()
+
+    def add_share(q):
+        slot = lax.rem(q, KEEP_OWN)
+        for h in range(2):
+            at1, _, p1, _ = places(h)
+            drain(recv1.at[q, h, pl.ds(0, 2)], got0.at[q, h])
+            after, before = (lax.rem(p1 + k, SIDE) * SIDE for k in (1, 3))
+            for j, start, k in ((0, after, 1), (1, before + PAIR, 3)):
+                total = own[slot, h, pl.ds(start, PAIR)] + recv1[q, h, j].astype(F32)
+                chain[q, h, j] = total.astype(BF16)
+                remote(
+                    chain.at[q, h, j], recv1.at[q, h, 4 + j],
                     send1.at[q, h], got1.at[q, h], at1(k),
                 ).start()
 
     def second(q):
         slot = lax.rem(q, KEEP)
-        for h in range(2):
-            _, at2, p1, p2 = places(h)
-            drain(recv1.at[q, h], got1.at[q, h])
-            total = own[slot, h, pl.ds(p1 * SIDE, SIDE)]
-            for k in range(SIDE - 1):
-                total = total + recv1[q, h, k].astype(F32)
-            mid_own[slot, h] = total
-            mid[q, h] = total.astype(BF16)
+        slot_own = lax.rem(q, KEEP_OWN)
+
+        for h in range(2):
+            p1 = places(h)[2]
+            drain(recv1.at[q, h, pl.ds(2, 4)], got1.at[q, h])
+            for half, j in ((0, (3, 4)), (1, (2, 5))):
+                total = own[slot_own, h, pl.ds(p1 * SIDE + half * PAIR, PAIR)]
+                for n in j:
+                    total = total + recv1[q, h, n].astype(F32)
+                mid_own[slot, h, pl.ds(half * PAIR, PAIR)] = total
+                mid[q, h, pl.ds(half * PAIR, PAIR)] = total.astype(BF16)
+
+        for h in range(2):
+            _, at2, _, p2 = places(h)
             for k in range(1, SIDE):
                 to = lax.rem(p2 + k, SIDE)
                 remote(
@@ -221,9 +247,19 @@
         for h in range(2):
             at1, _, p1, _ = places(h)
             drain(recv2.at[q, h], got3.at[q, h])
-            for k in range(1, SIDE):
-                block = full.at[q, h, pl.ds(p1 * SIDE, SIDE)]
+            block = full.at[q, h, pl.ds(p1 * SIDE, SIDE)]
+            for k in (1, 3):
                 remote(block, block, send4.at[q, h], got4.at[q, h], at1(k)).start()
+
+    def forward(q):
+        for h in range(2):
+            at1, _, p1, _ = places(h)
+            drain(recv1.at[q, h, pl.ds(0, 4)], got4.at[q, h])
+
+            after, before = (lax.rem(p1 + k, SIDE) * SIDE for k in (1, 3))
+            for start, k in ((before, 1), (after + PAIR, 3)):
+                block = full.at[q, h, pl.ds(start, PAIR)]
+                remote(block, block, send4.at[q, h], got5.at[q, h], at1(k)).start()
 
     def whole(q, n):
         return jnp.concatenate(
@@ -232,8 +268,8 @@
 
     def finish(q):
         th, r = half_of(q)
-        drain(recv1.at[q, 0], got4.at[q, 0])
-        drain(recv1.at[q, 1], got4.at[q, 1])
+        for h in range(2):
+            drain(recv1.at[q, h, pl.ds(0, 2)], got5.at[q, h])
         hidden, gate_grad, up_grad = whole(q, 0), whole(q, 1), whole(q, 2)
         half = TOK // 2
         value = dot(hidden, dw[r])
@@ -279,6 +315,8 @@
     def cores_start(th):
         cores_copy(th).start()
 
+    zsend, zrecv = (zsend_0, zsend_1), (zrecv_0, zrecv_1)
+
     def z_start(th):
         cores_copy(th).wait_recv()
         for k in order + (0,):
@@ -289,18 +327,18 @@
                 if k == 0:
                     zown[th, a] = value
                 else:
-                    zsend[th, k - 1, a] = value.astype(BF16)
+                    zsend[th][k - 1, a] = value.astype(zsend[th].dtype)
             if k:
                 remote(
-                    zsend.at[th, k - 1], zrecv.at[th, k - 1], z_send.at[th], z_recv.at[th], at_z(k)
+                    zsend[th].at[k - 1], zrecv[th].at[k - 1], z_send.at[th], z_recv.at[th], at_z(k)
                 ).start()
 
     def z_end(th):
-        drain(zrecv.at[th], z_recv.at[th])
+        drain(zrecv[th], z_recv.at[th])
         for a, out in enumerate((layer_out, grad_tokens)):
             value = zown[th, a]
             for k in range(ZS - 1):
-                value = value + zrecv[th, k, a].astype(F32)
+                value = value + zrecv[th][k, a].astype(F32)
             out[pl.ds(th * HALF, HALF)] = value.astype(BF16)
 
     @pl.loop(0, LAST)
@@ -310,9 +348,11 @@
             def _():
                 work(t - s * LAG)
 
-        stage(1, second)
-        stage(2, activations)
-        stage(3, spread)
+        stage(1, add_share)
+        stage(2, second)
+        stage(3, activations)
+        stage(4, spread)
+        stage(5, forward)
 
         @pl.when(t == NR - 1)
         def _():
@@ -329,13 +369,13 @@
             for th in range(2):
                 tok_t[th] = ab[th, :, 0].reshape(TOK, WID).T
 
-        stage(4, finish)
-
-        @pl.when(t >= NR + 4 * LAG)
+        stage(6, finish)
+
+        @pl.when(t >= NR + 6 * LAG)
         def _():
-            weight_grads(t - NR - 4 * LAG)
-
-        @pl.when(t == NR + 4 * LAG)
+            weight_grads(t - NR - 6 * LAG)
+
+        @pl.when(t == NR + 6 * LAG)
         def _():
             z_start(0)
 
@@ -344,7 +384,7 @@
     z_end(1)
 
     for th in range(2):
-        drain(zrecv.at[th], z_send.at[th])
+        drain(zrecv[th], z_send.at[th])
         cores_copy(th).wait_send()
         for k in range(ZS):
             if k:
@@ -404,29 +444,32 @@
             pltpu.VMEM((NR, WID, CH), BF16),
             pltpu.VMEM((NR, CH, WID), BF16),
             pltpu.VMEM((NQ, 2, GROUP) + block, BF16),
-            pltpu.VMEM((KEEP, 2, GROUP) + block, F32),
-            pltpu.VMEM((NQ, 2, SIDE - 1, SIDE) + block, BF16),
+            pltpu.VMEM((KEEP_OWN, 2, GROUP) + block, F32),
+            pltpu.VMEM((NQ, 2, 6, PAIR) + block, BF16),
             pltpu.VMEM((NQ, 2, SIDE) + block, BF16),
             pltpu.VMEM((KEEP, 2, SIDE) + block, F32),
             pltpu.VMEM((NQ, 2, SIDE - 1) + block, BF16),
             pltpu.VMEM((NQ, 2, GROUP) + block, BF16),
+            pltpu.VMEM((NQ, 2, 2, PAIR) + block, BF16),
             pltpu.VMEM((NR, WID, CH), BF16),
             pltpu.VMEM((NR, WID, CH), BF16),
             pltpu.VMEM((NR, CH, WID), BF16),
             pltpu.VMEM((2, 2, 2, TOK // 2, WID), F32),
             pltpu.VMEM((2, 2, TOK // 2, WID), F32),
-            pltpu.VMEM((2, ZS - 1, 2, HALF, WID), BF16),
             pltpu.VMEM((2, 2, HALF, WID), F32),
-            pltpu.VMEM((2, ZS - 1, 2, HALF, WID), BF16),
+            pltpu.VMEM((ZS - 1, 2, HALF, WID), F32),
+            pltpu.VMEM((ZS - 1, 2, HALF, WID), BF16),
+            pltpu.VMEM((ZS - 1, 2, HALF, WID), F32),
+            pltpu.VMEM((ZS - 1, 2, HALF, WID), BF16),
             dma((2, 2)),
             dma((3,)),
             dma((3, NR)),
             dma((2, ZS - 1)), dma((2, ZS - 1)),
             dma((2, ZS)), dma((2,)),
+            dma((NQ, 2)), dma((NQ, 2)), dma((NQ, 2)),
             dma((NQ, 2)), dma((NQ, 2)),
             dma((NQ, 2)), dma((NQ, 2)),
-            dma((NQ, 2)), dma((NQ, 2)),
-            dma((NQ, 2)), dma((NQ, 2)),
+            dma((NQ, 2)), dma((NQ, 2)), dma((NQ, 2)),
             dma((3, NR)),
             dma((2,)), dma((2,)), dma((2,)), dma((2,)),
         ],

time: 113 us -> 103 us (0.912)
  Pallas kernels: 113 us -> 102 us
    pallas_call x1, Pallas kernels: 110 us -> 99.6 us  [local(): pl.pallas_call(kernel, name='sparse_swiglu_step', out_shape=shapes, in_sp...]
where the time goes in v3:
time: 103 us
  Pallas kernels  102 us (99%)
    pallas_call x1, Pallas kernels, local(): pl.pallas_call(kernel, name='sparse_swiglu_step', out_shape=shapes, in_sp...  99.6 us
    pallas_call x1, Pallas kernels, local(): pl.pallas_call(hand_over, name='hand_over', out_shape=shapes, in_specs=[a...  2.5 us

profile of v3, /device:TPU:1, one launch (start us, length us, event | category | flops | bytes accessed | tf_op | source)
XLA Modules:
  0.0 102.7 jit_solution(15413783375317360773)
XLA Ops:
  0.6 99.6 %sparse_swiglu_step.1 = (bf16[32,512]{1,0:T(8,128)(2,1)S(1)}, bf16[32,512]{1,0:T(8,128)(2,1)S(1)}, bf16[512,1792]{1,0:T(8,128)(2,1)S(1)}, bf16[512,1792]{1,0:T(8,128)(2,1)S(1)}, bf16[1792,512]{1,0:T(8,128)(2,1)S(1)}) custom-call(bf16[32,512]{1,0:T(8,128)(2,1)} %tokens.1, bf16[32,512]{1,0:T(8,128)(2,1)} %grad_out.1, bf16[512,1792]{1,0:T(8,128)(2,1)} %gate_w.1, ...), custom_call_target="tpu_custom_call" | custom-call | tf_op jit(solution)/shard_map/sparse_swiglu_step/pallas_call | solution.py:431
  100.2 2.5 %hand_over.1 = (bf16[32,512]{1,0:T(8,128)(2,1)}, bf16[32,512]{1,0:T(8,128)(2,1)}, bf16[512,1792]{1,0:T(8,128)(2,1)}, bf16[512,1792]{1,0:T(8,128)(2,1)}, bf16[1792,512]{1,0:T(8,128)(2,1)}) custom-call(bf16[32,512]{1,0:T(8,128)(2,1)S(1)} %get-tuple-element.10.refs_0_, bf16[32,512]{1,0:T(8,128)(2,1)S(1)} %get-tuple-element.11.refs_1_, ...), custom_call_target="tpu_custom_call" | custom-call | tf_op jit(solution)/shard_map/hand_over/pallas_call | solution.py:485

commit v4 on v3

--- a/solution.py
+++ b/solution.py
@@ -23,11 +23,19 @@
 CH = 2 * LANES
 NR = HID // CH
 NQ = 2 * NR
-LAG = 2
+LAG = 3
 KEEP = LAG + 1
 KEEP_OWN = 2 * LAG + 1
 STAGES = 7
-LAST = NQ + (STAGES - 1) * LAG
+EARLY = 1
+WAIT = NR - EARLY
+LAST = NQ + WAIT + (STAGES - 1) * LAG
+NEAR = ((0, 0, 2, 0), (1, 2, 2, 0), (7, 4, 2, 0), (2, 6, 1, 0), (6, 7, 1, 0))
+FAR = ((3, 0, 2, 0), (5, 2, 2, 0), (4, 4, 2, 0), (2, 6, 1, 1), (6, 7, 1, 1))
+PIECES = (NEAR, FAR)
+WIDE = ((1, 2), (3, 4))
+ROWS_WIDE = ((2 * HALF, 4 * HALF), (6 * HALF, 2 * HALF))
+ROWS_NARROW = ((6 * HALF, 2 * HALF), (0, 6 * HALF))
 
 
 def dot(a, b):
@@ -46,7 +54,7 @@
     tokens, grad_out, gate_w, up_w, down_w, gate_mask, up_mask, down_mask,
     layer_out, grad_tokens, grad_gate, grad_up, grad_down,
     gate_m, up_m, down_m, ab, tok_t, gw, uw, dw, part, own, recv1, mid, mid_own, recv2, full,
-    chain, out_g, out_u, out_d, acc, xbuf, zown, zsend_0, zsend_1, zrecv_0, zrecv_1,
+    chain, out_g, out_u, out_d, acc, xbuf, zown, zsend_n, zsend_w, zrecv_n, zrecv_w,
     load_sem, m_sem, w_sem, a_send, a_recv, s_send, s_recv,
     send1, got0, got1, send2, got2, send3, got3, send4, got4, got5, out_sem,
     x_send, x_recv, z_send, z_recv,
@@ -77,26 +85,33 @@
     def drain(ref, sem):
         pltpu.make_async_copy(ref, ref, sem).wait()
 
-    mine = c * ZS + z
     first = []
-    for th in range(2):
-        rows = pl.ds(th * HALF, HALF)
-        first.append(pltpu.make_async_copy(tokens.at[rows], ab.at[th, mine, 0], load_sem.at[th, 0]))
-        first.append(pltpu.make_async_copy(grad_out.at[rows], ab.at[th, mine, 1], load_sem.at[th, 1]))
+    for half in range(2):
+        rows = pl.ds(half * HALF, HALF)
+        first.append(pltpu.make_async_copy(tokens.at[rows], ab.at[0, c * ZS + half, 0], load_sem.at[half, 0]))
+        first.append(pltpu.make_async_copy(grad_out.at[rows], ab.at[0, c * ZS + half, 1], load_sem.at[half, 1]))
     for copy in first:
         copy.start()
-    weights = [
+    masks = [
         pltpu.make_async_copy(gate_mask, gate_m, m_sem.at[0]),
         pltpu.make_async_copy(up_mask, up_m, m_sem.at[1]),
         pltpu.make_async_copy(down_mask, down_m, m_sem.at[2]),
     ]
-    for r in range(NR):
-        cols = pl.ds(r * CH, CH)
-        weights.append(pltpu.make_async_copy(gate_w.at[:, cols], gw.at[r], w_sem.at[0, r]))
-        weights.append(pltpu.make_async_copy(up_w.at[:, cols], uw.at[r], w_sem.at[1, r]))
-        weights.append(pltpu.make_async_copy(down_w.at[cols, :], dw.at[r], w_sem.at[2, r]))
-    for copy in weights:
+    for copy in masks:
         copy.start()
+
+    def weights(r):
+        cols = pl.ds(pl.multiple_of(r * CH, CH), CH)
+        return [
+            pltpu.make_async_copy(gate_w.at[:, cols], gw.at[r], w_sem.at[0, r]),
+            pltpu.make_async_copy(up_w.at[:, cols], uw.at[r], w_sem.at[1, r]),
+            pltpu.make_async_copy(down_w.at[cols, :], dw.at[r], w_sem.at[2, r]),
+        ]
+
+    @pl.loop(0, NR)
+    def _(r):
+        for copy in weights(r):
+            copy.start()
 
     barrier = pltpu.get_barrier_semaphore()
     for k in range(1, SIDE):
@@ -107,26 +122,31 @@
     pl.semaphore_signal(barrier, inc=1, device_id=sibling, device_id_type=MESH)
     pl.semaphore_wait(barrier, 2 * (SIDE - 1) + ZS - 1 + 1)
 
-    order = (4, 3, 5, 2, 6, 1, 7)
-    near = (1, 7, 2, 6, 3, 5, 4)
-
-    def z_copy(th, k):
-        block = ab.at[th, mine]
-        return remote(block, block, a_send.at[th, k - 1], a_recv.at[th, k - 1], at_z(k))
-
-    def to_sibling(th, k):
-        block = ab.at[th, c * ZS + lax.rem(z + ZS - k, ZS)]
-        return remote(block, block, s_send.at[th, k], s_recv.at[th], sibling)
+    def z_copy(th, p):
+        k, block, n, half = PIECES[th][p]
+        return remote(
+            ab.at[0, pl.ds(c * ZS + half, n)], ab.at[th, pl.ds(c * ZS + block, n)],
+            a_send.at[th, p], a_recv.at[th, p], at_z(ZS - k),
+        )
+
+    def to_sibling(th, p):
+        _, block, n, _ = PIECES[th][p]
+        part_of = ab.at[th, pl.ds(c * ZS + block, n)]
+        return remote(part_of, part_of, s_send.at[th, p], s_recv.at[th], sibling)
 
     def gather_start(th):
-        for k in order:
-            z_copy(th, k).start()
-        to_sibling(th, 0).start()
+        for p, piece in enumerate(PIECES[th]):
+            if piece[0]:
+                z_copy(th, p).start()
+        for p, piece in enumerate(PIECES[th]):
+            if not piece[0]:
+                to_sibling(th, p).start()
 
     def gather_relay(th):
-        for k in near:
-            z_copy(th, k).wait_recv()
-            to_sibling(th, k).start()
+        for p, piece in enumerate(PIECES[th]):
+            if piece[0]:
+                z_copy(th, p).wait_recv()
+                to_sibling(th, p).start()
 
     def gather_end(th):
         drain(ab.at[th, pl.ds(sib * ZS, ZS)], s_recv.at[th])
@@ -136,9 +156,12 @@
     gather_start(0)
 
     acc[...] = jnp.zeros_like(acc)
-    for copy in weights:
+    for copy in masks:
         copy.wait()
-    for r in range(NR):
+
+    def mask_weights(r):
+        for copy in weights(r):
+            copy.wait()
         for a in range(WID // LANES):
             for b in range(2):
                 rows, cols = pl.ds(a * LANES, LANES), pl.ds(b * LANES, LANES)
@@ -148,6 +171,7 @@
                 keep = jnp.full((LANES, LANES), down_m[a, 2 * r + b].astype(F32), F32)
                 dw[r, cols, rows] = dw[r, cols, rows] * keep.astype(BF16)
 
+    mask_weights(0)
     gather_relay(0)
     gather_end(0)
     gather_start(1)
@@ -204,9 +228,8 @@
     def second(q):
         slot = lax.rem(q, KEEP)
         slot_own = lax.rem(q, KEEP_OWN)
-
-        for h in range(2):
-            p1 = places(h)[2]
+        for h in range(2):
+            _, at2, p1, p2 = places(h)
             drain(recv1.at[q, h, pl.ds(2, 4)], got1.at[q, h])
             for half, j in ((0, (3, 4)), (1, (2, 5))):
                 total = own[slot_own, h, pl.ds(p1 * SIDE + half * PAIR, PAIR)]
@@ -214,9 +237,6 @@
                     total = total + recv1[q, h, n].astype(F32)
                 mid_own[slot, h, pl.ds(half * PAIR, PAIR)] = total
                 mid[q, h, pl.ds(half * PAIR, PAIR)] = total.astype(BF16)
-
-        for h in range(2):
-            _, at2, _, p2 = places(h)
             for k in range(1, SIDE):
                 to = lax.rem(p2 + k, SIDE)
                 remote(
@@ -255,7 +275,6 @@
         for h in range(2):
             at1, _, p1, _ = places(h)
             drain(recv1.at[q, h, pl.ds(0, 4)], got4.at[q, h])
-
             after, before = (lax.rem(p1 + k, SIDE) * SIDE for k in (1, 3))
             for start, k in ((before, 1), (after + PAIR, 3)):
                 block = full.at[q, h, pl.ds(start, PAIR)]
@@ -279,9 +298,13 @@
         acc[th, 0, 1] += value[:half]
         acc[th, 1, 1] += value[half:]
 
-        @pl.when(r == NR - 1)
-        def _():
-            cores_start(th)
+        @pl.when(q == NR - 1)
+        def _():
+            cores_start(0)
+
+        @pl.when(q == NQ - 1)
+        def _():
+            cores_start(1)
 
     def weight_grads(r):
         for out, n, m in ((out_g, 1, gate_m), (out_u, 2, up_m)):
@@ -309,37 +332,57 @@
             pltpu.make_async_copy(out_d.at[r], grad_down.at[cols, :], out_sem.at[2, r]),
         ]
 
-    def cores_copy(th):
-        return remote(acc.at[th, sib], xbuf.at[th], x_send.at[th], x_recv.at[th], sibling)
+    def z_buffers(th, p):
+        wide = p in WIDE[th]
+        return (zsend_w, zrecv_w, 1) if wide else (zsend_n, zrecv_n, 0)
+
+    outward = ((3, 4, 1, 2, 0), (2, 0, 1, 3, 4))
+
+    def rows_of(th, p):
+        _, block, n, _ = PIECES[th][p]
+        return pl.ds(block * HALF, n * HALF)
+
+    def cores_copy(th, p):
+        rows = rows_of(th, p)
+        return remote(
+            acc.at[th, sib, :, rows], xbuf.at[th, :, rows], x_send.at[th, p], x_recv.at[th, p], sibling
+        )
 
     def cores_start(th):
-        cores_copy(th).start()
-
-    zsend, zrecv = (zsend_0, zsend_1), (zrecv_0, zrecv_1)
+        for p in outward[th]:
+            cores_copy(th, p).start()
 
     def z_start(th):
-        cores_copy(th).wait_recv()
-        for k in order + (0,):
-            to = lax.rem(z + k, ZS)
-            rows = pl.ds(pl.multiple_of(to * HALF, HALF), HALF)
+        for p in outward[th]:
+            cores_copy(th, p).wait_recv()
+            k, rows = PIECES[th][p][0], rows_of(th, p)
+            zsend, zrecv, kind = z_buffers(th, p)
             for a in range(2):
                 value = acc[th, c, a, rows] + xbuf[th, a, rows]
                 if k == 0:
-                    zown[th, a] = value
+                    zown[a] = value
                 else:
-                    zsend[th][k - 1, a] = value.astype(zsend[th].dtype)
+                    zsend[th, a, rows] = value.astype(zsend.dtype)
             if k:
                 remote(
-                    zsend[th].at[k - 1], zrecv[th].at[k - 1], z_send.at[th], z_recv.at[th], at_z(k)
+                    zsend.at[th, :, rows], zrecv.at[th, :, rows],
+                    z_send.at[th, kind], z_recv.at[th, kind], at_z(k),
                 ).start()
 
-    def z_end(th):
-        drain(zrecv[th], z_recv.at[th])
+    def z_bytes(th, sem):
+        drain(zrecv_n.at[th, :, pl.ds(*ROWS_NARROW[th])], sem.at[th, 0])
+        drain(zrecv_w.at[th, :, pl.ds(*ROWS_WIDE[th])], sem.at[th, 1])
+
+    def results():
         for a, out in enumerate((layer_out, grad_tokens)):
-            value = zown[th, a]
-            for k in range(ZS - 1):
-                value = value + zrecv[th][k, a].astype(F32)
-            out[pl.ds(th * HALF, HALF)] = value.astype(BF16)
+            for half in range(2):
+                value = zown[a, pl.ds(half * HALF, HALF)]
+                for th in (1, 0):
+                    for p, (k, block, n, start) in enumerate(PIECES[th]):
+                        if k and start <= half < start + n:
+                            rows = pl.ds((block + half - start) * HALF, HALF)
+                            value = value + z_buffers(th, p)[1][th, a, rows].astype(F32)
+                out[pl.ds(half * HALF, HALF)] = value.astype(BF16)
 
     @pl.loop(0, LAST)
     def _(t):
@@ -351,8 +394,18 @@
         stage(1, add_share)
         stage(2, second)
         stage(3, activations)
-        stage(4, spread)
-        stage(5, forward)
+
+        def gathered(s, work):
+            j = t - WAIT - s * LAG
+
+            @pl.when(jnp.logical_and(j >= 0, j < NQ))
+            def _():
+                past_early = lax.div(j + NQ - EARLY, NQ)
+                past_other = lax.div(j + NQ - EARLY - NR, NQ)
+                work(j + WAIT * past_early - (WAIT + NR) * past_other)
+
+        gathered(4, spread)
+        gathered(5, forward)
 
         @pl.when(t == NR - 1)
         def _():
@@ -364,32 +417,44 @@
 
         stage(0, partial_sums)
 
-        @pl.when(t == NR + 1)
+        @pl.when(t < NR - 1)
+        def _():
+            mask_weights(t + 1)
+
+
+        @pl.when(t == NR + 2)
         def _():
             for th in range(2):
                 tok_t[th] = ab[th, :, 0].reshape(TOK, WID).T
 
-        stage(6, finish)
-
-        @pl.when(t >= NR + 6 * LAG)
-        def _():
-            weight_grads(t - NR - 6 * LAG)
-
-        @pl.when(t == NR + 6 * LAG)
-        def _():
-            z_start(0)
-
-    z_start(1)
-    z_end(0)
-    z_end(1)
+        gathered(6, finish)
+        j = t - WAIT - 6 * LAG
+
+        @pl.when(jnp.logical_and(j >= EARLY, j < 2 * EARLY))
+        def _():
+            weight_grads(j - EARLY)
+
+        @pl.when(jnp.logical_and(j >= NR + EARLY, j < NQ))
+        def _():
+            weight_grads(j - NR)
+
+        @pl.when(j == NR + EARLY)
+        def _():
+            z_start(1)
+
+    z_start(0)
+    z_bytes(1, z_recv)
+    z_bytes(0, z_recv)
+    results()
 
     for th in range(2):
-        drain(zrecv[th], z_send.at[th])
-        cores_copy(th).wait_send()
-        for k in range(ZS):
-            if k:
-                z_copy(th, k).wait_send()
-            to_sibling(th, k).wait_send()
+        z_bytes(th, z_send)
+        for p in range(5):
+            cores_copy(th, p).wait_send()
+        for p, piece in enumerate(PIECES[th]):
+            if piece[0]:
+                z_copy(th, p).wait_send()
+            to_sibling(th, p).wait_send()
 
     @pl.loop(0, NQ)
     def _(q):
@@ -456,22 +521,22 @@
             pltpu.VMEM((NR, CH, WID), BF16),
             pltpu.VMEM((2, 2, 2, TOK // 2, WID), F32),
             pltpu.VMEM((2, 2, TOK // 2, WID), F32),
-            pltpu.VMEM((2, 2, HALF, WID), F32),
-            pltpu.VMEM((ZS - 1, 2, HALF, WID), F32),
-            pltpu.VMEM((ZS - 1, 2, HALF, WID), BF16),
-            pltpu.VMEM((ZS - 1, 2, HALF, WID), F32),
-            pltpu.VMEM((ZS - 1, 2, HALF, WID), BF16),
+            pltpu.VMEM((2, ROWS, WID), F32),
+            pltpu.VMEM((2, 2, ZS * HALF, WID), BF16),
+            pltpu.VMEM((2, 2, ZS * HALF, WID), F32),
+            pltpu.VMEM((2, 2, ZS * HALF, WID), BF16),
+            pltpu.VMEM((2, 2, ZS * HALF, WID), F32),
             dma((2, 2)),
             dma((3,)),
             dma((3, NR)),
-            dma((2, ZS - 1)), dma((2, ZS - 1)),
-            dma((2, ZS)), dma((2,)),
+            dma((2, 5)), dma((2, 5)),
+            dma((2, 5)), dma((2,)),
             dma((NQ, 2)), dma((NQ, 2)), dma((NQ, 2)),
             dma((NQ, 2)), dma((NQ, 2)),
             dma((NQ, 2)), dma((NQ, 2)),
             dma((NQ, 2)), dma((NQ, 2)), dma((NQ, 2)),
             dma((3, NR)),
-            dma((2,)), dma((2,)), dma((2,)), dma((2,)),
+            dma((2, 5)), dma((2, 5)), dma((2, 2)), dma((2, 2)),
         ],
         compiler_params=pltpu.CompilerParams(
             collective_id=0, has_side_effects=True, vmem_limit_bytes=48 << 20

time: 103 us -> 99.5 us (0.966)
  Pallas kernels: 102 us -> 98.8 us
    pallas_call x1, Pallas kernels: 99.6 us -> 96.3 us  [local(): pl.pallas_call(kernel, name='sparse_swiglu_step', out_shape=shapes, in_sp...]
where the time goes in v4:
time: 99.5 us; the launch traced here: 99.4 us
  Pallas kernels  98.8 us (99%)
    pallas_call x1, Pallas kernels, local(): pl.pallas_call(kernel, name='sparse_swiglu_step', out_shape=shapes, in_sp...  96.3 us
    pallas_call x1, Pallas kernels, local(): pl.pallas_call(hand_over, name='hand_over', out_shape=shapes, in_specs=[a...  2.5 us

profile of v4, /device:TPU:1, one launch (start us, length us, event | category | flops | bytes accessed | tf_op | source)
XLA Modules:
  0.0 99.4 jit_solution(18195426536989624545)
XLA Ops:
  0.6 96.3 %sparse_swiglu_step.1 = (bf16[32,512]{1,0:T(8,128)(2,1)S(1)}, bf16[32,512]{1,0:T(8,128)(2,1)S(1)}, bf16[512,1792]{1,0:T(8,128)(2,1)S(1)}, bf16[512,1792]{1,0:T(8,128)(2,1)S(1)}, bf16[1792,512]{1,0:T(8,128)(2,1)S(1)}) custom-call(bf16[32,512]{1,0:T(8,128)(2,1)} %tokens.1, bf16[32,512]{1,0:T(8,128)(2,1)} %grad_out.1, bf16[512,1792]{1,0:T(8,128)(2,1)} %gate_w.1, ...), custom_call_target="tpu_custom_call" | custom-call | tf_op jit(solution)/shard_map/sparse_swiglu_step/pallas_call | solution.py:496
  96.9 2.5 %hand_over.1 = (bf16[32,512]{1,0:T(8,128)(2,1)}, bf16[32,512]{1,0:T(8,128)(2,1)}, bf16[512,1792]{1,0:T(8,128)(2,1)}, bf16[512,1792]{1,0:T(8,128)(2,1)}, bf16[1792,512]{1,0:T(8,128)(2,1)}) custom-call(bf16[32,512]{1,0:T(8,128)(2,1)S(1)} %get-tuple-element.10.refs_0_, bf16[32,512]{1,0:T(8,128)(2,1)S(1)} %get-tuple-element.11.refs_1_, ...), custom_call_target="tpu_custom_call" | custom-call | tf_op jit(solution)/shard_map/hand_over/pallas_call | solution.py:550

commit v5 on v4

--- a/solution.py
+++ b/solution.py
@@ -85,6 +85,14 @@
     def drain(ref, sem):
         pltpu.make_async_copy(ref, ref, sem).wait()
 
+    barrier = pltpu.get_barrier_semaphore()
+    for k in range(1, SIDE):
+        pl.semaphore_signal(barrier, inc=1, device_id=at_x(k), device_id_type=MESH)
+        pl.semaphore_signal(barrier, inc=1, device_id=at_y(k), device_id_type=MESH)
+    for k in range(1, ZS):
+        pl.semaphore_signal(barrier, inc=1, device_id=at_z(k), device_id_type=MESH)
+    pl.semaphore_signal(barrier, inc=1, device_id=sibling, device_id_type=MESH)
+
     first = []
     for half in range(2):
         rows = pl.ds(half * HALF, HALF)
@@ -113,13 +121,6 @@
         for copy in weights(r):
             copy.start()
 
-    barrier = pltpu.get_barrier_semaphore()
-    for k in range(1, SIDE):
-        pl.semaphore_signal(barrier, inc=1, device_id=at_x(k), device_id_type=MESH)
-        pl.semaphore_signal(barrier, inc=1, device_id=at_y(k), device_id_type=MESH)
-    for k in range(1, ZS):
-        pl.semaphore_signal(barrier, inc=1, device_id=at_z(k), device_id_type=MESH)
-    pl.semaphore_signal(barrier, inc=1, device_id=sibling, device_id_type=MESH)
     pl.semaphore_wait(barrier, 2 * (SIDE - 1) + ZS - 1 + 1)
 
     def z_copy(th, p):
@@ -135,8 +136,8 @@
         return remote(part_of, part_of, s_send.at[th, p], s_recv.at[th], sibling)
 
     def gather_start(th):
-        for p, piece in enumerate(PIECES[th]):
-            if piece[0]:
+        for p in (3, 4, 2, 1, 0):
+            if PIECES[th][p][0]:
                 z_copy(th, p).start()
         for p, piece in enumerate(PIECES[th]):
             if not piece[0]:
@@ -473,7 +474,15 @@
 def hand_over(*refs):
     n = len(refs) // 2
     sem = refs[-1]
-    copies = [pltpu.make_async_copy(refs[j], refs[n + j], sem.at[j]) for j in range(n)]
+    copies = []
+    for j in range(n):
+        rows = refs[j].shape[0]
+        step = rows if rows == ROWS else rows // 4
+        for k in range(0, rows, step):
+            part = pl.ds(k, step)
+            copies.append(
+                pltpu.make_async_copy(refs[j].at[part], refs[n + j].at[part], sem.at[len(copies)])
+            )
     for copy in copies:
         copy.start()
     for copy in copies:
@@ -553,7 +562,7 @@
         out_shape=shapes,
         in_specs=[any_spec] * 5,
         out_specs=[any_spec] * 5,
-        scratch_shapes=[dma((5,))],
+        scratch_shapes=[dma((14,))],
         compiler_params=pltpu.CompilerParams(vmem_limit_bytes=1 << 20),
     )(*results)
 

time: 99.5 us -> 98.6 us (level)
  no operation moved by 1% of the time
where the time goes in v5:
time: 98.6 us
  Pallas kernels  97.9 us (99%)
    pallas_call x1, Pallas kernels, local(): pl.pallas_call(kernel, name='sparse_swiglu_step', out_shape=shapes, in_sp...  95.4 us
    pallas_call x1, Pallas kernels, local(): pl.pallas_call(hand_over, name='hand_over', out_shape=shapes, in_specs=[a...  2.55 us

profile of v5, /device:TPU:1, one launch (start us, length us, event | category | flops | bytes accessed | tf_op | source)
XLA Modules:
  0.0 98.6 jit_solution(13930375088140837298)
XLA Ops:
  0.6 95.4 %sparse_swiglu_step.1 = (bf16[32,512]{1,0:T(8,128)(2,1)S(1)}, bf16[32,512]{1,0:T(8,128)(2,1)S(1)}, bf16[512,1792]{1,0:T(8,128)(2,1)S(1)}, bf16[512,1792]{1,0:T(8,128)(2,1)S(1)}, bf16[1792,512]{1,0:T(8,128)(2,1)S(1)}) custom-call(bf16[32,512]{1,0:T(8,128)(2,1)} %tokens.1, bf16[32,512]{1,0:T(8,128)(2,1)} %grad_out.1, bf16[512,1792]{1,0:T(8,128)(2,1)} %gate_w.1, ...), custom_call_target="tpu_custom_call" | custom-call | tf_op jit(solution)/shard_map/sparse_swiglu_step/pallas_call | solution.py:505
  96.0 2.5 %hand_over.1 = (bf16[32,512]{1,0:T(8,128)(2,1)}, bf16[32,512]{1,0:T(8,128)(2,1)}, bf16[512,1792]{1,0:T(8,128)(2,1)}, bf16[512,1792]{1,0:T(8,128)(2,1)}, bf16[1792,512]{1,0:T(8,128)(2,1)}) custom-call(bf16[32,512]{1,0:T(8,128)(2,1)S(1)} %get-tuple-element.10.refs_0_, bf16[32,512]{1,0:T(8,128)(2,1)S(1)} %get-tuple-element.11.refs_1_, ...), custom_call_target="tpu_custom_call" | custom-call | tf_op jit(solution)/shard_map/hand_over/pallas_call | solution.py:559
